TPU v7x, 128 devices: a whole 4x4x4 slice. The times are simulated.
128 devices in a mesh: ha: 8 (over z_lo, x), wa: 16 (over z_hi, y, core).
Axes of the slice: x: 4, y: 4, z: 4 (z_hi: 2, z_lo: 2; z = z_hi * 2 + z_lo), core: 2. Of those that a mesh axis runs over, the one named last changes fastest.
Arguments:
- field: bfloat16 [384, 1024, 256], P('ha', 'wa'), may hold values from -41 to 41
- expand_w: bfloat16 [256, 1024], replicated, may hold values from -0.375 to 0.375
- dw_kernel: float32 [9, 1024], replicated, may hold values from -2 to 2
- project_w: bfloat16 [1024, 256], replicated, may hold values from -0.1875 to 0.1875
- blk_qkv: bfloat16 [256, 768], replicated, may hold values from -0.375 to 0.375
- blk_out: bfloat16 [256, 256], replicated, may hold values from -0.375 to 0.375
- blk_table: float32 [225, 8], replicated, may hold values from -4 to 290
- blk_index: int32 [64, 64], replicated, may hold values from 0 to 224, as said below
- blk_up: bfloat16 [256, 1024], replicated, may hold values from -0.375 to 0.375
- blk_down: bfloat16 [1024, 256], replicated, may hold values from -0.1875 to 0.1875
- grid_qkv: bfloat16 [256, 768], replicated, may hold values from -0.375 to 0.375
- grid_out: bfloat16 [256, 256], replicated, may hold values from -0.375 to 0.375
- grid_table: float32 [225, 8], replicated, may hold values from -4 to 290
- grid_index: int32 [64, 64], replicated, may hold values from 0 to 224, as said below
- grid_up: bfloat16 [256, 1024], replicated, may hold values from -0.375 to 0.375
- grid_down: bfloat16 [1024, 256], replicated, may hold values from -0.1875 to 0.1875
Outputs:
- updated: bfloat16 [384, 1024, 256], P('ha', 'wa')
Inputs may be any that keep to these rules, and one draw needn't show every extreme that they name: `blk_index`: two entries are equal exactly when their query and key positions differ by the same row and column offsets inside the window. `grid_index`: two entries are equal exactly when their query and key positions differ by the same row and column offsets inside the window.
All inputs are finite; a program needn't handle non-finite values.
Results may differ from a plain program's by a relative error of at most 0.013.
Values may be sent and summed in bfloat16 or wider, within the bound.
No kernel may reach another device: no remote copies, remote signals or barrier semaphores. Data moves between devices by JAX's collectives and lax.ppermute only.
A program may use at most 128 MiB of HBM per device.

v0:
```python
import functools
import math

import jax
import jax.numpy as jnp
from jax import lax
from jax.experimental import pallas as pl
from jax.experimental.pallas import tpu as pltpu
from jax.sharding import Mesh
from jax.sharding import PartitionSpec as P

EPS = 1e-05
LOG2E = 1.4426950408889634
C0 = 0.7978845608028654
C1 = C0 * 0.044715
F32 = jnp.float32
BF16 = jnp.bfloat16
WIDE = 80
CHUNKS = (6,)
PARAMS = pltpu.CompilerParams(vmem_limit_bytes=56 << 20)


def norm(x):
    center = x - jnp.sum(x, axis=-1, keepdims=True) * (1.0 / 256.0)
    spread = jnp.sum(center * center, axis=-1, keepdims=True) * (1.0 / 256.0)
    return (center * lax.rsqrt(spread + EPS)).astype(BF16)


def gelu2(v):
    v = v.astype(BF16)
    u = v * (jnp.asarray(C1, BF16) * (v * v) + jnp.asarray(C0, BF16))
    return v + v * jnp.tanh(u)


def mm(a, b):
    return jnp.dot(a, b, preferred_element_type=F32)


def mm_nt(a, b):
    return lax.dot_general(a, b, (((1,), (1,)), ((), ())), preferred_element_type=F32)


def make_bias(table_ref, index_ref, bias_ref):
    index = index_ref[...]
    low = lax.broadcasted_iota(jnp.int32, (64, 128), 1) < 64
    upper = index >= 128
    within = jnp.bitwise_and(index, 127)
    got = []
    for h in range(8):
        halves = []
        for half in range(2):
            row = jnp.broadcast_to(table_ref[h : h + 1, 128 * half : 128 * half + 128] * LOG2E, (64, 128))
            halves.append(jnp.take_along_axis(row, within, axis=1))
        got.append(jnp.where(upper, halves[1], halves[0]))
    for h in range(0, 8, 2):
        g, c = h // 4, (h % 4) // 2
        lanes = slice(128 * c, 128 * c + 128)
        bias_ref[g, 0:64, lanes] = jnp.where(low, got[h], got[h + 1])
        bias_ref[g, 64:128, lanes] = jnp.where(low, got[h + 1], got[h])


def attend(windows, n_ref, qkv_ref, wt_ref, bias_ref, k_ref, qvt_ref, o_ref, s_refs, e_refs, d_refs):
    scale = LOG2E / math.sqrt(32.0)
    block = 64 * windows // 2

    def maps(i, carry):
        rows = pl.ds(pl.multiple_of(block * i, 256), block)
        k_ref[rows] = mm(n_ref[rows], qkv_ref[:, 256:512]).astype(BF16)
        qvt_ref[:, rows] = mm_nt(wt_ref[...], n_ref[rows]).astype(BF16)
        return carry

    lax.fori_loop(0, 2, maps, 0)
    lane = lax.broadcasted_iota(jnp.int32, (1, 128), 1)
    low = lane < 64
    even = (lane // 32) % 2 == 0
    lowm = low.astype(BF16)
    highm = (lane >= 64).astype(BF16)
    groups = windows // 4

    def place(i, u):
        g = u % 2
        return g, slice(128 * g, 128 * g + 128), pl.multiple_of(256 * i + 128 * (u // 2), 128)

    def scores(i, u):
        g, cols, rows = place(i, u)
        qt = qvt_ref[cols, pl.ds(rows, 128)]
        turn = pltpu.roll(qt.astype(F32), 64, 1).astype(BF16)
        zero = jnp.zeros((32, 128), BF16)
        for side in range(2):
            straight = qt * (lowm if side == 0 else highm)
            rolled = turn * (highm if side == 0 else lowm)
            blocks = []
            for c in range(2):
                parts = [zero] * 4
                parts[2 * c] = straight[64 * c : 64 * c + 32]
                parts[2 * c + 1] = rolled[64 * c + 32 : 64 * c + 64]
                blocks.append(jnp.concatenate(parts, axis=0))
            keys = k_ref[pl.ds(rows + 64 * side, 64), cols]
            s_refs[u][64 * side : 64 * side + 64, :] = mm(keys, jnp.concatenate(blocks, axis=1))

    def soften(u):
        g = u % 2
        for side in range(2):
            rows = slice(64 * side, 64 * side + 64)
            for c in range(2):
                lanes = slice(128 * c, 128 * c + 128)
                s = s_refs[u][rows, lanes] * scale + bias_ref[g, rows, lanes]
                e = jnp.exp2(s - jnp.max(s, axis=0, keepdims=True))
                d_refs[u][side : side + 1, lanes] = 1.0 / jnp.sum(e, axis=0, keepdims=True)
                e_refs[u][rows, lanes] = e.astype(BF16)

    def mix(i, u):
        g, cols, rows = place(i, u)
        vt = qvt_ref[256 + 128 * g : 256 + 128 * g + 128, pl.ds(rows, 128)]
        r = mm(jnp.concatenate([vt * lowm, vt * highm], axis=0), e_refs[u][...])
        parts = []
        for j in range(4):
            lanes = slice(128 * (j // 2), 128 * (j // 2) + 128)
            a, b = r[32 * j : 32 * j + 32, lanes], r[128 + 32 * j : 128 + 32 * j + 32, lanes]
            da, db = d_refs[u][0:1, lanes], d_refs[u][1:2, lanes]
            if j % 2 == 1:
                a, b, da, db = b, a, db, da
            parts.append(jnp.where(low, a, b) * jnp.where(low, da, db))
        t = jnp.concatenate(parts, axis=0).T
        o = jnp.concatenate(
            [jnp.where(even, t[0:64], t[64:128]), jnp.where(even, t[64:128], t[0:64])], axis=0
        )
        o_ref[pl.ds(rows, 128), cols] = o.astype(BF16)

    def turn(i, stages):
        for step in range(6):
            if "mix" in stages and step < 4:
                mix(i - 1, step)
            if "soften" in stages and 1 <= step < 5:
                soften(step - 1)
            if "scores" in stages and step >= 2:
                scores(i + 1, step - 2)

    turn(-1, ("scores",))
    turn(0, ("soften", "scores"))

    def body(i, carry):
        turn(i, ("mix", "soften", "scores"))
        return carry

    lax.fori_loop(1, groups - 1, body, 0)
    turn(groups - 1, ("mix", "soften"))
    turn(groups, ("mix",))


def project_and_feed(x_ref, o_ref, g_ref, n_ref, out_w_ref, up_ref, down_ref, y_ref):
    block = x_ref.shape[0] // 2

    def half(i, carry):
        rows = pl.ds(pl.multiple_of(block * i, 256), block)
        y = x_ref[rows] + mm(o_ref[rows], out_w_ref[...])
        x_ref[rows] = y
        n_ref[rows] = norm(y)
        for p in range(4):
            lanes = slice(256 * p, 256 * p + 256)
            g_ref[:, lanes] = gelu2(mm(n_ref[rows], up_ref[:, lanes])).astype(BF16)
        y_ref[rows] = x_ref[rows] + 0.5 * mm(g_ref[...], down_ref[...])
        return carry

    lax.fori_loop(0, 2, half, 0)


def local_kernel(
    first, strips,
    x_ref, above_ref, below_ref, left_ref, right_ref,
    ew_ref, dw_ref, pw_ref, qkv_ref, wt_ref, table_ref, index_ref, out_w_ref, up_ref, down_ref,
    res_ref,
    hid0_ref, hid1_ref, act0_ref, act1_ref, xn_ref,
    bias_ref, xw_ref, n_ref, k_ref, qvt_ref, o_ref, g_ref, y_ref, *units
):
    rows = 8 * strips
    last = x_ref.shape[0]
    hids, acts = (hid0_ref, hid1_ref), (act0_ref, act1_ref)
    make_bias(table_ref, index_ref, bias_ref)

    for r in range(2):
        image = 8 * first + r - 1
        x = above_ref[0] if image < 0 else x_ref[image]
        xn_ref[64 * r : 64 * r + 64] = norm(x.astype(F32))
    for i, ref in enumerate((left_ref, right_ref)):
        xn_ref[128 + 64 * i : 128 + 64 * i + rows + 2] = norm(
            ref[8 * first : 8 * first + rows + 2].astype(F32)
        )

    def normalize(strip, carry):
        x = x_ref[pl.ds(8 * (first + strip) + 1, 8)].reshape(512, 256)
        xn_ref[pl.ds(pl.multiple_of(512 * strip + 256, 256), 512)] = norm(x.astype(F32))
        return carry

    ends = 8 * (first + strips) >= last
    lax.fori_loop(0, strips - 1 if ends else strips, normalize, 0)
    if ends:
        at = 512 * (strips - 1) + 256
        x = x_ref[last - 7 : last].reshape(448, 256)
        xn_ref[at : at + 448] = norm(x.astype(F32))
        xn_ref[at + 448 : at + 512] = norm(below_ref[0].astype(F32))

    def hidden_border(p, hid):
        h = gelu2(mm(xn_ref[0:256], ew_ref[:, 256 * p : 256 * p + 256])).astype(F32)
        for c in range(2):
            lanes = slice(128 * c, 128 * c + 128)
            hid[c, 0:2, 8:72, :] = h[0:128, lanes].reshape(2, 64, 128)
            for r in range(rows + 2):
                hid[c, r, 7:8, :] = h[128 + r : 129 + r, lanes]
                hid[c, r, 72:73, :] = h[192 + r : 193 + r, lanes]

    def hidden_part(p, hid, strip, part):
        at = pl.multiple_of(512 * strip + 256 + 256 * part, 256)
        h = gelu2(mm(xn_ref[pl.ds(at, 256)], ew_ref[:, 256 * p : 256 * p + 256])).astype(F32)
        for c in range(2):
            lanes = slice(128 * c, 128 * c + 128)
            hid[c, pl.ds(8 * strip + 2 + 4 * part, 4), 8:72, :] = h[:, lanes].reshape(4, 64, 128)

    def project_part(p, act, strip, part):
        at = pl.ds(pl.multiple_of(512 * strip + 256 * part, 256), 256)
        d = mm(act[at], pw_ref[256 * p : 256 * p + 256, :])
        y_ref[at] = d if p == 0 else y_ref[at] + d

    def conv_part(p, hid, act, strip, c, half):
        w = (dw_ref[:, 256 * p + 128 * c : 256 * p + 128 * c + 128] * 0.5).astype(BF16)
        begin = 7 + 32 * half
        acc = [None] * 8
        for ir in range(10):
            h = [hid[c, 8 * strip + ir, begin + d : begin + d + 32, :].astype(BF16) for d in range(3)]
            for dy in range(3):
                orow = ir - dy
                if 0 <= orow < 8:
                    t = h[0] * w[3 * dy : 3 * dy + 1] + h[1] * w[3 * dy + 1 : 3 * dy + 2]
                    t = t + h[2] * w[3 * dy + 2 : 3 * dy + 3]
                    acc[orow] = t if acc[orow] is None else acc[orow] + t
            if ir >= 2:
                to = pl.multiple_of(512 * strip + 64 * (ir - 2) + 32 * half, 32)
                act[pl.ds(to, 32), 128 * c : 128 * c + 128] = gelu2(acc[ir - 2])

    def first_hidden(strip, carry):
        for part in range(2):
            hidden_part(0, hids[0], strip, part)
        return carry

    hidden_border(0, hids[0])
    lax.fori_loop(0, strips, first_hidden, 0)
    for p in range(4):
        if p < 3:
            hidden_border(p + 1, hids[(p + 1) % 2])

        def quarter(strip, carry, p=p):
            for c in range(2):
                for half in range(2):
                    if half == 0 and p < 3:
                        hidden_part(p + 1, hids[(p + 1) % 2], strip, c)
                    if half == 1 and p > 0:
                        project_part(p - 1, acts[(p - 1) % 2], strip, c)
                    conv_part(p, hids[p % 2], acts[p % 2], strip, c, half)
            return carry

        lax.fori_loop(0, strips, quarter, 0)

    def gather(strip, carry):
        at = pl.ds(pl.multiple_of(512 * strip, 512), 512)
        x = x_ref[pl.ds(8 * (first + strip), 8)].reshape(512, 256).astype(F32)
        y = y_ref[at] + mm(acts[1][at], pw_ref[768:1024, :])
        y = (x + 0.5 * y).reshape(8, 64, 256)
        for w in range(8):
            to = pl.ds(pl.multiple_of(512 * strip + 64 * w, 64), 64)
            x = y[:, 8 * w : 8 * w + 8].reshape(64, 256)
            xw_ref[to] = x
            n_ref[to] = norm(x)
        return carry

    lax.fori_loop(0, strips, gather, 0)
    attend(8 * strips, n_ref, qkv_ref, wt_ref, bias_ref, k_ref, qvt_ref, o_ref, units[0:4], units[4:8], units[8:12])
    project_and_feed(xw_ref, o_ref, g_ref, n_ref, out_w_ref, up_ref, down_ref, y_ref)

    def spread(strip, carry):
        for w in range(8):
            y = y_ref[pl.ds(pl.multiple_of(512 * strip + 64 * w, 64), 64)]
            res_ref[pl.ds(8 * strip, 8), 8 * w : 8 * w + 8, :] = y.reshape(8, 8, 256).astype(BF16)
        return carry

    lax.fori_loop(0, strips, spread, 0)


def grid_kernel(
    windows,
    x_ref, qkv_ref, wt_ref, table_ref, index_ref, out_w_ref, up_ref, down_ref,
    res_ref,
    xs_ref, bias_ref, xw_ref, n_ref, k_ref, qvt_ref, o_ref, g_ref, y_ref, *units
):
    make_bias(table_ref, index_ref, bias_ref)
    x = x_ref[...].astype(F32).reshape(64 * windows, 256)
    xs_ref[0] = x[:, 0:128]
    xs_ref[1] = x[:, 128:256]
    for w in range(windows):
        rows = slice(64 * w, 64 * w + 64)
        for half in range(2):
            xw_ref[rows, 128 * half : 128 * half + 128] = xs_ref[half, pl.ds(w, 64, stride=windows), :]
    n_ref[...] = norm(xw_ref[...])
    attend(windows, n_ref, qkv_ref, wt_ref, bias_ref, k_ref, qvt_ref, o_ref, units[0:4], units[4:8], units[8:12])
    project_and_feed(xw_ref, o_ref, g_ref, n_ref, out_w_ref, up_ref, down_ref, y_ref)
    for w in range(windows):
        rows = slice(64 * w, 64 * w + 64)
        for half in range(2):
            xs_ref[half, pl.ds(w, 64, stride=windows), :] = y_ref[rows, 128 * half : 128 * half + 128]
    y = jnp.concatenate([xs_ref[0], xs_ref[1]], axis=1)
    res_ref[...] = y.reshape(64, windows, 256).astype(BF16)


def attend_scratch(windows):
    rows = 64 * windows
    return [
        pltpu.VMEM((2, 128, 256), F32),
        pltpu.VMEM((rows, 256), F32),
        pltpu.VMEM((rows, 256), BF16),
        pltpu.VMEM((rows, 256), BF16),
        pltpu.VMEM((512, rows), BF16),
        pltpu.VMEM((rows, 256), BF16),
        pltpu.VMEM((rows // 2, 1024), BF16),
        pltpu.VMEM((rows, 256), F32),
    ] + [pltpu.VMEM((128, 256), F32)] * 4 + [pltpu.VMEM((128, 256), BF16)] * 4 + [pltpu.VMEM((2, 256), F32)] * 4


def in_vmem(count):
    return [pl.BlockSpec(memory_space=pltpu.VMEM)] * count


def local_stage(first, strips, cells, weights):
    ops = tuple(cells) + tuple(weights)
    rows = 8 * strips
    return pl.pallas_call(
        functools.partial(local_kernel, first, strips),
        in_specs=in_vmem(len(ops)),
        out_specs=in_vmem(1)[0],
        out_shape=jax.ShapeDtypeStruct((rows, 64, 256), BF16),
        scratch_shapes=[
            pltpu.VMEM((2, rows + 2, WIDE, 128), F32),
            pltpu.VMEM((2, rows + 2, WIDE, 128), F32),
            pltpu.VMEM((64 * rows, 256), BF16),
            pltpu.VMEM((64 * rows, 256), BF16),
            pltpu.VMEM((64 * rows + 256, 256), BF16),
        ]
        + attend_scratch(8 * strips),
        compiler_params=PARAMS,
        name="local_stage",
    )(*ops)


def grid_stage(x, weights):
    windows = x.shape[1]
    ops = (x,) + tuple(weights)
    return pl.pallas_call(
        functools.partial(grid_kernel, windows),
        in_specs=in_vmem(len(ops)),
        out_specs=in_vmem(1)[0],
        out_shape=jax.ShapeDtypeStruct(x.shape, BF16),
        scratch_shapes=[pltpu.VMEM((2, 64 * windows, 128), F32)] + attend_scratch(windows),
        compiler_params=PARAMS,
        name="grid_stage",
    )(*ops)


def bias_operands(table, index):
    turned_index = index.T
    return (
        jnp.pad(table.T, ((0, 0), (0, 256 - table.shape[0]))),
        jnp.concatenate([turned_index, turned_index], axis=1),
    )


def turned(qkv):
    return jnp.concatenate([qkv[:, :256], qkv[:, 512:]], axis=1).T


def neighbours(before, after, axes):
    count = lax.axis_size(axes)
    up = [(i, i + 1) for i in range(count - 1)]
    down = [(j, i) for i, j in up]
    return lax.ppermute(before, axes, up), lax.ppermute(after, axes, down)


def on_device(
    field, expand_w, dw_kernel, project_w,
    blk_qkv, blk_out, blk_table, blk_index, blk_up, blk_down,
    grid_qkv, grid_out, grid_table, grid_index, grid_up, grid_down,
):
    rows, cols, width = field.shape
    above, below = neighbours(field[-1:], field[:1], "ha")
    first = jnp.concatenate([above[:, 0], field[:, 0], below[:, 0]], axis=0)
    final = jnp.concatenate([above[:, -1], field[:, -1], below[:, -1]], axis=0)
    left, right = neighbours(final, first, ("wh", "core"))
    cells = (field, above, below, left, right)
    local_w = (expand_w, dw_kernel, project_w, blk_qkv, turned(blk_qkv))
    local_w += bias_operands(blk_table, blk_index) + (blk_out, blk_up, blk_down)
    grid_w = (grid_qkv, turned(grid_qkv)) + bias_operands(grid_table, grid_index)
    grid_w += (grid_out, grid_up, grid_down)
    outs = []
    start = 0
    for strips in CHUNKS:
        part = local_stage(start, strips, cells, local_w)
        start += strips
        part = part.reshape(64, strips * 8, width)
        moved = lax.all_to_all(part, ("ha", "wh"), 0, 0, tiled=True)
        done = grid_stage(moved, grid_w)
        back = lax.all_to_all(done, ("ha", "wh"), 0, 0, tiled=True)
        outs.append(back.reshape(strips * 8, cols, width))
    return outs[0] if len(outs) == 1 else jnp.concatenate(outs, axis=0)


def solution(mesh):
    split = Mesh(mesh.devices.reshape(8, 8, 2), ("ha", "wh", "core"))
    spec = P("ha", ("wh", "core"), None)
    return jax.shard_map(
        on_device, mesh=split, in_specs=(spec,) + (P(),) * 15, out_specs=spec, check_vma=False
    )
```

profile of v0, /device:TPU:0, one launch (start us, length us, event | category | flops | bytes accessed | tf_op | source)
XLA Modules:
  0.0 137.9 jit_solution(8940401746465011890)
XLA Ops:
  0.0 0.8 fusion.1
  0.8 3.5 %collective-permute-start = (bf16[1,64,256]{2,1,0:T(8,128)(2,1)S(1)}, bf16[1,64,256]{2,1,0:T(8,128)(2,1)S(1)}, u32[]{:S(2)}, u32[]{:S(2)}) collective-permute-start(bf16[1,64,256]{2,1,0:T(8,128)(2,1)S(1)} %get-tuple-element.8), channel_id=1, source_target_pairs={{0,16},{16,32},{32,48},{48,64},{64,80},{80,96},{96,112},{1,17},{17... | collective-permute-start | bytes 98312 | tf_op jit(solution)/shard_map/ppermute | solution.py:382
  4.3 1.3 collective-permute-start.1
  5.6 1.1 fusion
  6.7 1.0 fusion.3
  7.9 0.7 maximum_bitcast_fusion.wt_ref
  8.7 1.3 collective-permute-done.1.below_ref
  10.1 1.3 collective-permute-start.3
  11.4 3.0 %collective-permute-start.2 = (bf16[50,256]{1,0:T(8,128)(2,1)S(1)}, bf16[50,256]{1,0:T(8,128)(2,1)S(1)}, u32[]{:S(2)}, u32[]{:S(2)}) collective-permute-start(bf16[50,256]{1,0:T(8,128)(2,1)S(1)} %pad_maximum_fusion), channel_id=1, source_target_pairs={{0,1},{1,2},{2,3},{3,4},{4,5},{5,6},{6,7},{7,8},{8,9},{9,10},{10,1... | collective-permute-start | bytes 76808 | tf_op jit(solution)/shard_map/ppermute | solution.py:382
  14.5 0.7 pad_add_fusion.index_ref
  15.2 0.6 pad.7.table_ref
  15.8 0.6 copy-done.6
  16.4 0.6 copy-done.7
  17.0 33.8 %local_stage.1 = bf16[48,64,256]{2,1,0:T(8,128)(2,1)} custom-call(bf16[48,64,256]{2,1,0:T(8,128)(2,1)} %x_ref.1, bf16[1,64,256]{2,1,0:T(8,128)(2,1)} %copy-done.2, bf16[1,64,256]{2,1,0:T(8,128)(2,1)} %copy-done.3, bf16[50,256]{1,0:T(8,128)(2,1)} %copy-done.7, bf16[50,256]{1,0:T(8,128)(2,1)} %copy-done.6, bf16[256,1024]{1,0:T(8,128)(2,1)} %ew_ref.1, ...), custom_call_target="tpu_custom_call" | custom-call | tf_op jit(solution)/shard_map/local_stage/pallas_call | solution.py:334
  50.8 15.7 %all-to-all-start = ((bf16[64,48,256]{2,1,0:T(8,128)(2,1)}), bf16[64,48,256]{2,1,0:T(8,128)(2,1)S(1)}, u32[]{:S(2)}, u32[]{:S(2)}) async-start(bf16[64,48,256]{2,1,0:T(8,128)(2,1)} %bitcast.25), calls=%async_computation | async-start | bytes 3145728 | tf_op jit(solution)/shard_map/all_to_all | solution.py:406
  66.5 0.1 copy.29
  66.8 0.6 pad.8.table_ref
  67.4 0.7 pad_add_fusion.1.index_ref
  68.1 0.7 maximum_bitcast_fusion.1.wt_ref
  68.8 20.0 %all-to-all-done.x_ref = bf16[64,48,256]{2,1,0:T(8,128)(2,1)S(1)} async-done(((bf16[64,48,256]{2,1,0:T(8,128)(2,1)}), bf16[64,48,256]{2,1,0:T(8,128)(2,1)S(1)}, u32[]{:S(2)}, u32[]{:S(2)}) %all-to-all-start) | async-done | bytes 1572896 | tf_op jit(solution)/shard_map/all_to_all | solution.py:406
  88.8 1.1 copy-done
  89.9 19.2 %grid_stage.1 = bf16[64,48,256]{2,1,0:T(8,128)(2,1)} custom-call(bf16[64,48,256]{2,1,0:T(8,128)(2,1)} %copy-done, bf16[256,768]{1,0:T(8,128)(2,1)} %qkv_ref.3, bf16[512,256]{1,0:T(8,128)(2,1)} %maximum_bitcast_fusion.1.wt_ref, f32[8,256]{1,0:T(8,128)} %pad.8.table_ref, s32[64,128]{1,0:T(8,128)} %pad_add_fusion.1.index_ref, bf16[256,256]{1,0:T(8,128)(2,1)} %out_w_ref.3, ...), custom_call_target="tpu_custom_call" | custom-call | tf_op jit(solution)/shard_map/grid_stage/pallas_call | solution.py:355
  109.2 27.6 %all_to_all.10 = bf16[64,48,256]{2,1,0:T(8,128)(2,1)S(1)} all-to-all(bf16[64,48,256]{2,1,0:T(8,128)(2,1)} %grid_stage.1), channel_id=1, replica_groups=mesh['ha'=8,'wh'=8,'core'=2] {'ha','wh'}, dimensions={0} | all-to-all | bytes 3145728 | tf_op jit(solution)/shard_map/all_to_all | solution.py:408
  136.7 1.1 copy.36
  (32 shorter events, 0.6 us)
Async XLA Ops:
  0.0 8.6 %copy-start.4 = (s32[64,64]{1,0:T(8,128)S(1)}, s32[64,64]{1,0:T(8,128)}, u32[]{:S(2)}) copy-start(s32[64,64]{1,0:T(8,128)} %param.23) | copy-start | bytes 49156
  0.0 15.2 %copy-start.8 = (f32[225,8]{0,1:T(8,128)S(1)}, f32[225,8]{0,1:T(8,128)}, u32[]{:S(2)}) copy-start(f32[225,8]{0,1:T(8,128)} %param.22) | copy-start | bytes 21604
  0.8 7.9 %collective-permute-start = (bf16[1,64,256]{2,1,0:T(8,128)(2,1)S(1)}, bf16[1,64,256]{2,1,0:T(8,128)(2,1)S(1)}, u32[]{:S(2)}, u32[]{:S(2)}) collective-permute-start(bf16[1,64,256]{2,1,0:T(8,128)(2,1)S(1)} %get-tuple-element.8), channel_id=1, source_target_pairs={{0,16},{16,32},{32,48},{48,64},{64,80},{80,96},{96,112},{1,17},{17... | collective-permute-start | bytes 98312 | tf_op jit(solution)/shard_map/ppermute | solution.py:382
  4.3 5.8 %collective-permute-start.1 = (bf16[1,64,256]{2,1,0:T(8,128)(2,1)S(1)}, bf16[1,64,256]{2,1,0:T(8,128)(2,1)S(1)}, u32[]{:S(2)}, u32[]{:S(2)}) collective-permute-start(bf16[1,64,256]{2,1,0:T(8,128)(2,1)S(1)} %get-tuple-element.7), channel_id=1, source_target_pairs={{16,0},{32,16},{48,32},{64,48},{80,64},{96,80},{112,96},{17,1},{33... | collective-permute-start | bytes 98312 | tf_op jit(solution)/shard_map/ppermute | solution.py:382
  8.7 7.1 %copy-start.2 = (bf16[1,64,256]{2,1,0:T(8,128)(2,1)}, bf16[1,64,256]{2,1,0:T(8,128)(2,1)S(1)}, u32[]{:S(2)}) copy-start(bf16[1,64,256]{2,1,0:T(8,128)(2,1)S(1)} %collective-permute-done.above_ref) | copy-start | bytes 98308
  10.1 5.7 %copy-start.3 = (bf16[1,64,256]{2,1,0:T(8,128)(2,1)}, bf16[1,64,256]{2,1,0:T(8,128)(2,1)S(1)}, u32[]{:S(2)}) copy-start(bf16[1,64,256]{2,1,0:T(8,128)(2,1)S(1)} %collective-permute-done.1.below_ref) | copy-start | bytes 98308
  10.1 5.6 %collective-permute-start.3 = (bf16[50,256]{1,0:T(8,128)(2,1)S(1)}, bf16[50,256]{1,0:T(8,128)(2,1)S(1)}, u32[]{:S(2)}, u32[]{:S(2)}) collective-permute-start(bf16[50,256]{1,0:T(8,128)(2,1)S(1)} %pad_maximum_fusion.1), channel_id=1, source_target_pairs={{1,0},{2,1},{3,2},{4,3},{5,4},{6,5},{7,6},{8,7},{9,8},{10,9},{11,1... | collective-permute-start | bytes 76808 | tf_op jit(solution)/shard_map/ppermute | solution.py:382
  11.4 4.3 %collective-permute-start.2 = (bf16[50,256]{1,0:T(8,128)(2,1)S(1)}, bf16[50,256]{1,0:T(8,128)(2,1)S(1)}, u32[]{:S(2)}, u32[]{:S(2)}) collective-permute-start(bf16[50,256]{1,0:T(8,128)(2,1)S(1)} %pad_maximum_fusion), channel_id=1, source_target_pairs={{0,1},{1,2},{2,3},{3,4},{4,5},{5,6},{6,7},{7,8},{8,9},{9,10},{10,1... | collective-permute-start | bytes 76808 | tf_op jit(solution)/shard_map/ppermute | solution.py:382
  15.8 0.6 copy-start.6
  16.4 0.6 copy-start.7
  50.7 15.8 %copy-start.1 = (bf16[256,768]{1,0:T(8,128)(2,1)S(1)}, bf16[256,768]{1,0:T(8,128)(2,1)}, u32[]{:S(2)}) copy-start(bf16[256,768]{1,0:T(8,128)(2,1)} %qkv_ref.3) | copy-start | bytes 1179652
  50.7 16.0 %copy-start.5 = (s32[64,64]{1,0:T(8,128)S(1)}, s32[64,64]{1,0:T(8,128)}, u32[]{:S(2)}) copy-start(s32[64,64]{1,0:T(8,128)} %param.29) | copy-start | bytes 49156
  50.7 16.1 %copy-start.9 = (f32[225,8]{0,1:T(8,128)S(1)}, f32[225,8]{0,1:T(8,128)}, u32[]{:S(2)}) copy-start(f32[225,8]{0,1:T(8,128)} %param.28) | copy-start | bytes 21604
  50.8 38.1 %all-to-all-start = ((bf16[64,48,256]{2,1,0:T(8,128)(2,1)}), bf16[64,48,256]{2,1,0:T(8,128)(2,1)S(1)}, u32[]{:S(2)}, u32[]{:S(2)}) async-start(bf16[64,48,256]{2,1,0:T(8,128)(2,1)} %bitcast.25), calls=%async_computation | async-start | bytes 3145728 | tf_op jit(solution)/shard_map/all_to_all | solution.py:406
  88.8 1.1 copy-start
where the time goes:
time: 138 us
  Pallas kernels  53 us (38%)
  blocking collectives  27.6 us (20%)
  starting transfers between devices  24.8 us (18%)
  waiting for transfers between devices  21.3 us (15%)
  local copies, waits for them, and re-layouts  8.15 us (6%)
  other arithmetic  2.82 us (2%)
    pallas_call x1, Pallas kernels, local_stage(): pl.pallas_call(functools.partial(local_kernel, first, strips), in_specs=i...  33.8 us
    all_to_all x1, blocking collectives, on_device(): back = lax.all_to_all(done, ('ha', 'wh'), 0, 0, tiled=True)  27.6 us
    all_to_all x1, waiting for transfers between devices, on_device(): moved = lax.all_to_all(part, ('ha', 'wh'), 0, 0, tiled=True)  20 us
    pallas_call x1, Pallas kernels, grid_stage(): pl.pallas_call(functools.partial(grid_kernel, windows), in_specs=in_vmem(...  19.2 us
    all_to_all x1, starting transfers between devices, on_device(): moved = lax.all_to_all(part, ('ha', 'wh'), 0, 0, tiled=True)  15.7 us
    ppermute x4, starting transfers between devices, neighbours(): return (lax.ppermute(before, axes, up), lax.ppermute(after, axes, down))  9.08 us
    unnamed x29, local copies, waits for them, and re-layouts  4.04 us
  transfers between devices with their start and end apart: 5, of which 2 were waited for; matrix products, arithmetic and copies ran while one was open for 5% of the time, Pallas kernels for 0%

commit v1 on v0

--- a/solution.py
+++ b/solution.py
@@ -16,6 +16,7 @@
 F32 = jnp.float32
 BF16 = jnp.bfloat16
 WIDE = 80
+UNITS = 8
 CHUNKS = (6,)
 PARAMS = pltpu.CompilerParams(vmem_limit_bytes=56 << 20)
 
@@ -38,6 +39,16 @@
 
 def mm_nt(a, b):
     return lax.dot_general(a, b, (((1,), (1,)), ((), ())), preferred_element_type=F32)
+
+
+def fetch(sources, targets, sems):
+    copies = [
+        pltpu.make_async_copy(source, target, sems.at[i])
+        for i, (source, target) in enumerate(zip(sources, targets))
+    ]
+    for copy in copies:
+        copy.start()
+    return copies
 
 
 def make_bias(table_ref, index_ref, bias_ref):
@@ -75,11 +86,11 @@
     even = (lane // 32) % 2 == 0
     lowm = low.astype(BF16)
     highm = (lane >= 64).astype(BF16)
-    groups = windows // 4
+    groups = windows // UNITS
 
     def place(i, u):
         g = u % 2
-        return g, slice(128 * g, 128 * g + 128), pl.multiple_of(256 * i + 128 * (u // 2), 128)
+        return g, slice(128 * g, 128 * g + 128), pl.multiple_of(64 * UNITS * i + 128 * (u // 2), 128)
 
     def scores(i, u):
         g, cols, rows = place(i, u)
@@ -128,10 +139,10 @@
         o_ref[pl.ds(rows, 128), cols] = o.astype(BF16)
 
     def turn(i, stages):
-        for step in range(6):
-            if "mix" in stages and step < 4:
+        for step in range(UNITS + 2):
+            if "mix" in stages and step < UNITS:
                 mix(i - 1, step)
-            if "soften" in stages and 1 <= step < 5:
+            if "soften" in stages and 1 <= step < UNITS + 1:
                 soften(step - 1)
             if "scores" in stages and step >= 2:
                 scores(i + 1, step - 2)
@@ -168,14 +179,16 @@
 def local_kernel(
     first, strips,
     x_ref, above_ref, below_ref, left_ref, right_ref,
-    ew_ref, dw_ref, pw_ref, qkv_ref, wt_ref, table_ref, index_ref, out_w_ref, up_ref, down_ref,
-    res_ref,
-    hid0_ref, hid1_ref, act0_ref, act1_ref, xn_ref,
-    bias_ref, xw_ref, n_ref, k_ref, qvt_ref, o_ref, g_ref, y_ref, *units
+    ew_ref, dw_ref, table_ref, index_ref, *rest
 ):
+    late, rest = rest[:6], rest[6:]
+    res_ref, hid_ref, act_ref, xn_ref, sems = rest[:5]
+    pw_ref, qkv_ref, wt_ref, out_w_ref, up_ref, down_ref = rest[5:11]
+    bias_ref, xw_ref, n_ref, k_ref, qvt_ref, o_ref, g_ref, y_ref = rest[11:19]
+    units = rest[19:]
+    copies = fetch(late, rest[5:11], sems)
     rows = 8 * strips
     last = x_ref.shape[0]
-    hids, acts = (hid0_ref, hid1_ref), (act0_ref, act1_ref)
     make_bias(table_ref, index_ref, bias_ref)
 
     for r in range(2):
@@ -200,33 +213,30 @@
         xn_ref[at : at + 448] = norm(x.astype(F32))
         xn_ref[at + 448 : at + 512] = norm(below_ref[0].astype(F32))
 
-    def hidden_border(p, hid):
+    def hidden_border(p):
         h = gelu2(mm(xn_ref[0:256], ew_ref[:, 256 * p : 256 * p + 256])).astype(F32)
         for c in range(2):
             lanes = slice(128 * c, 128 * c + 128)
-            hid[c, 0:2, 8:72, :] = h[0:128, lanes].reshape(2, 64, 128)
+            hid_ref[c, 0:2, 8:72, :] = h[0:128, lanes].reshape(2, 64, 128)
             for r in range(rows + 2):
-                hid[c, r, 7:8, :] = h[128 + r : 129 + r, lanes]
-                hid[c, r, 72:73, :] = h[192 + r : 193 + r, lanes]
-
-    def hidden_part(p, hid, strip, part):
-        at = pl.multiple_of(512 * strip + 256 + 256 * part, 256)
-        h = gelu2(mm(xn_ref[pl.ds(at, 256)], ew_ref[:, 256 * p : 256 * p + 256])).astype(F32)
+                hid_ref[c, r, 7:8, :] = h[128 + r : 129 + r, lanes]
+                hid_ref[c, r, 72:73, :] = h[192 + r : 193 + r, lanes]
+
+    def hidden_part(p, part):
+        at = pl.multiple_of(256 * strips * part + 256, 256)
+        h = gelu2(mm(xn_ref[pl.ds(at, 256 * strips)], ew_ref[:, 256 * p : 256 * p + 256])).astype(F32)
         for c in range(2):
             lanes = slice(128 * c, 128 * c + 128)
-            hid[c, pl.ds(8 * strip + 2 + 4 * part, 4), 8:72, :] = h[:, lanes].reshape(4, 64, 128)
-
-    def project_part(p, act, strip, part):
-        at = pl.ds(pl.multiple_of(512 * strip + 256 * part, 256), 256)
-        d = mm(act[at], pw_ref[256 * p : 256 * p + 256, :])
-        y_ref[at] = d if p == 0 else y_ref[at] + d
-
-    def conv_part(p, hid, act, strip, c, half):
+            hid_ref[c, pl.ds(4 * strips * part + 2, 4 * strips), 8:72, :] = h[:, lanes].reshape(
+                4 * strips, 64, 128
+            )
+
+    def conv_part(p, strip, c, half):
         w = (dw_ref[:, 256 * p + 128 * c : 256 * p + 128 * c + 128] * 0.5).astype(BF16)
         begin = 7 + 32 * half
         acc = [None] * 8
         for ir in range(10):
-            h = [hid[c, 8 * strip + ir, begin + d : begin + d + 32, :].astype(BF16) for d in range(3)]
+            h = [hid_ref[c, 8 * strip + ir, begin + d : begin + d + 32, :].astype(BF16) for d in range(3)]
             for dy in range(3):
                 orow = ir - dy
                 if 0 <= orow < 8:
@@ -235,36 +245,34 @@
                     acc[orow] = t if acc[orow] is None else acc[orow] + t
             if ir >= 2:
                 to = pl.multiple_of(512 * strip + 64 * (ir - 2) + 32 * half, 32)
-                act[pl.ds(to, 32), 128 * c : 128 * c + 128] = gelu2(acc[ir - 2])
-
-    def first_hidden(strip, carry):
-        for part in range(2):
-            hidden_part(0, hids[0], strip, part)
-        return carry
-
-    hidden_border(0, hids[0])
-    lax.fori_loop(0, strips, first_hidden, 0)
+                lanes = slice(256 * p + 128 * c, 256 * p + 128 * c + 128)
+                act_ref[pl.ds(to, 32), lanes] = gelu2(acc[ir - 2])
+
     for p in range(4):
-        if p < 3:
-            hidden_border(p + 1, hids[(p + 1) % 2])
-
-        def quarter(strip, carry, p=p):
+        hidden_border(p)
+
+        def hidden(part, carry, p=p):
+            hidden_part(p, part)
+            return carry
+
+        def conv(strip, carry, p=p):
             for c in range(2):
                 for half in range(2):
-                    if half == 0 and p < 3:
-                        hidden_part(p + 1, hids[(p + 1) % 2], strip, c)
-                    if half == 1 and p > 0:
-                        project_part(p - 1, acts[(p - 1) % 2], strip, c)
-                    conv_part(p, hids[p % 2], acts[p % 2], strip, c, half)
+                    conv_part(p, strip, c, half)
             return carry
 
-        lax.fori_loop(0, strips, quarter, 0)
+        lax.fori_loop(0, 2, hidden, 0)
+        lax.fori_loop(0, strips, conv, 0)
+
+    def project(part, carry):
+        at = pl.ds(pl.multiple_of(256 * strips * part, 256), 256 * strips)
+        y_ref[at] = mm(act_ref[at], pw_ref[...])
+        return carry
 
     def gather(strip, carry):
         at = pl.ds(pl.multiple_of(512 * strip, 512), 512)
         x = x_ref[pl.ds(8 * (first + strip), 8)].reshape(512, 256).astype(F32)
-        y = y_ref[at] + mm(acts[1][at], pw_ref[768:1024, :])
-        y = (x + 0.5 * y).reshape(8, 64, 256)
+        y = (x + 0.5 * y_ref[at]).reshape(8, 64, 256)
         for w in range(8):
             to = pl.ds(pl.multiple_of(512 * strip + 64 * w, 64), 64)
             x = y[:, 8 * w : 8 * w + 8].reshape(64, 256)
@@ -272,8 +280,14 @@
             n_ref[to] = norm(x)
         return carry
 
+    copies[0].wait()
+    lax.fori_loop(0, 2, project, 0)
     lax.fori_loop(0, strips, gather, 0)
-    attend(8 * strips, n_ref, qkv_ref, wt_ref, bias_ref, k_ref, qvt_ref, o_ref, units[0:4], units[4:8], units[8:12])
+    for copy in copies[1:3]:
+        copy.wait()
+    attend(8 * strips, n_ref, qkv_ref, wt_ref, bias_ref, k_ref, qvt_ref, o_ref, units[:UNITS], units[UNITS : 2 * UNITS], units[2 * UNITS :])
+    for copy in copies[3:]:
+        copy.wait()
     project_and_feed(xw_ref, o_ref, g_ref, n_ref, out_w_ref, up_ref, down_ref, y_ref)
 
     def spread(strip, carry):
@@ -287,10 +301,11 @@
 
 def grid_kernel(
     windows,
-    x_ref, qkv_ref, wt_ref, table_ref, index_ref, out_w_ref, up_ref, down_ref,
+    x_ref, qkv_ref, wt_ref, table_ref, index_ref, late0_ref, late1_ref, late2_ref,
     res_ref,
-    xs_ref, bias_ref, xw_ref, n_ref, k_ref, qvt_ref, o_ref, g_ref, y_ref, *units
+    xs_ref, sems, out_w_ref, up_ref, down_ref, bias_ref, xw_ref, n_ref, k_ref, qvt_ref, o_ref, g_ref, y_ref, *units
 ):
+    copies = fetch((late0_ref, late1_ref, late2_ref), (out_w_ref, up_ref, down_ref), sems)
     make_bias(table_ref, index_ref, bias_ref)
     x = x_ref[...].astype(F32).reshape(64 * windows, 256)
     xs_ref[0] = x[:, 0:128]
@@ -300,7 +315,9 @@
         for half in range(2):
             xw_ref[rows, 128 * half : 128 * half + 128] = xs_ref[half, pl.ds(w, 64, stride=windows), :]
     n_ref[...] = norm(xw_ref[...])
-    attend(windows, n_ref, qkv_ref, wt_ref, bias_ref, k_ref, qvt_ref, o_ref, units[0:4], units[4:8], units[8:12])
+    attend(windows, n_ref, qkv_ref, wt_ref, bias_ref, k_ref, qvt_ref, o_ref, units[:UNITS], units[UNITS : 2 * UNITS], units[2 * UNITS :])
+    for copy in copies:
+        copy.wait()
     project_and_feed(xw_ref, o_ref, g_ref, n_ref, out_w_ref, up_ref, down_ref, y_ref)
     for w in range(windows):
         rows = slice(64 * w, 64 * w + 64)
@@ -308,6 +325,9 @@
             xs_ref[half, pl.ds(w, 64, stride=windows), :] = y_ref[rows, 128 * half : 128 * half + 128]
     y = jnp.concatenate([xs_ref[0], xs_ref[1]], axis=1)
     res_ref[...] = y.reshape(64, windows, 256).astype(BF16)
+
+
+UNIT_SCRATCH = (((128, 256), F32), ((128, 256), BF16), ((2, 256), F32))
 
 
 def attend_scratch(windows):
@@ -321,43 +341,50 @@
         pltpu.VMEM((rows, 256), BF16),
         pltpu.VMEM((rows // 2, 1024), BF16),
         pltpu.VMEM((rows, 256), F32),
-    ] + [pltpu.VMEM((128, 256), F32)] * 4 + [pltpu.VMEM((128, 256), BF16)] * 4 + [pltpu.VMEM((2, 256), F32)] * 4
+    ] + [pltpu.VMEM(shape, kind) for shape, kind in UNIT_SCRATCH for _ in range(UNITS)]
+
+
+def landing(arrays):
+    return [pltpu.SemaphoreType.DMA((len(arrays),))] + [pltpu.VMEM(a.shape, a.dtype) for a in arrays]
+
+
+def in_hbm(count):
+    return [pl.BlockSpec(memory_space=pl.ANY)] * count
 
 
 def in_vmem(count):
     return [pl.BlockSpec(memory_space=pltpu.VMEM)] * count
 
 
-def local_stage(first, strips, cells, weights):
-    ops = tuple(cells) + tuple(weights)
+def local_stage(first, strips, cells, early, late):
+    ops = tuple(cells) + tuple(early) + tuple(late)
     rows = 8 * strips
     return pl.pallas_call(
         functools.partial(local_kernel, first, strips),
-        in_specs=in_vmem(len(ops)),
+        in_specs=in_vmem(len(cells) + len(early)) + in_hbm(len(late)),
         out_specs=in_vmem(1)[0],
         out_shape=jax.ShapeDtypeStruct((rows, 64, 256), BF16),
         scratch_shapes=[
             pltpu.VMEM((2, rows + 2, WIDE, 128), F32),
-            pltpu.VMEM((2, rows + 2, WIDE, 128), F32),
-            pltpu.VMEM((64 * rows, 256), BF16),
-            pltpu.VMEM((64 * rows, 256), BF16),
+            pltpu.VMEM((64 * rows, 1024), BF16),
             pltpu.VMEM((64 * rows + 256, 256), BF16),
         ]
+        + landing(late)
         + attend_scratch(8 * strips),
         compiler_params=PARAMS,
         name="local_stage",
     )(*ops)
 
 
-def grid_stage(x, weights):
+def grid_stage(x, early, late):
     windows = x.shape[1]
-    ops = (x,) + tuple(weights)
+    ops = (x,) + tuple(early) + tuple(late)
     return pl.pallas_call(
         functools.partial(grid_kernel, windows),
-        in_specs=in_vmem(len(ops)),
+        in_specs=in_vmem(1 + len(early)) + in_hbm(len(late)),
         out_specs=in_vmem(1)[0],
         out_shape=jax.ShapeDtypeStruct(x.shape, BF16),
-        scratch_shapes=[pltpu.VMEM((2, 64 * windows, 128), F32)] + attend_scratch(windows),
+        scratch_shapes=[pltpu.VMEM((2, 64 * windows, 128), F32)] + landing(late) + attend_scratch(windows),
         compiler_params=PARAMS,
         name="grid_stage",
     )(*ops)
@@ -393,18 +420,18 @@
     final = jnp.concatenate([above[:, -1], field[:, -1], below[:, -1]], axis=0)
     left, right = neighbours(final, first, ("wh", "core"))
     cells = (field, above, below, left, right)
-    local_w = (expand_w, dw_kernel, project_w, blk_qkv, turned(blk_qkv))
-    local_w += bias_operands(blk_table, blk_index) + (blk_out, blk_up, blk_down)
+    local_w = (expand_w, dw_kernel) + bias_operands(blk_table, blk_index)
+    local_late = (project_w, blk_qkv, turned(blk_qkv), blk_out, blk_up, blk_down)
     grid_w = (grid_qkv, turned(grid_qkv)) + bias_operands(grid_table, grid_index)
-    grid_w += (grid_out, grid_up, grid_down)
+    grid_late = (grid_out, grid_up, grid_down)
     outs = []
     start = 0
     for strips in CHUNKS:
-        part = local_stage(start, strips, cells, local_w)
+        part = local_stage(start, strips, cells, local_w, local_late)
         start += strips
         part = part.reshape(64, strips * 8, width)
         moved = lax.all_to_all(part, ("ha", "wh"), 0, 0, tiled=True)
-        done = grid_stage(moved, grid_w)
+        done = grid_stage(moved, grid_w, grid_late)
         back = lax.all_to_all(done, ("ha", "wh"), 0, 0, tiled=True)
         outs.append(back.reshape(strips * 8, cols, width))
     return outs[0] if len(outs) == 1 else jnp.concatenate(outs, axis=0)

time: 138 us -> 134 us (0.971)
  Pallas kernels: 53 us -> 48.9 us
    pallas_call x1, Pallas kernels: 33.8 us -> 30.9 us  [local_stage(): pl.pallas_call(functools.partial(local_kernel, first, strips), in_specs=i...]
where the time goes in v1:
time: 134 us
  Pallas kernels  48.9 us (36%)
  blocking collectives  27.5 us (21%)
  starting transfers between devices  24.7 us (18%)
  waiting for transfers between devices  21.5 us (16%)
  local copies, waits for them, and re-layouts  8.15 us (6%)
  other arithmetic  2.82 us (2%)
    pallas_call x1, Pallas kernels, local_stage(): pl.pallas_call(functools.partial(local_kernel, first, strips), in_specs=i...  30.9 us
    all_to_all x1, blocking collectives, on_device(): back = lax.all_to_all(done, ('ha', 'wh'), 0, 0, tiled=True)  27.5 us
    all_to_all x1, waiting for transfers between devices, on_device(): moved = lax.all_to_all(part, ('ha', 'wh'), 0, 0, tiled=True)  20.1 us
    pallas_call x1, Pallas kernels, grid_stage(): pl.pallas_call(functools.partial(grid_kernel, windows), in_specs=in_vmem(...  18 us
    all_to_all x1, starting transfers between devices, on_device(): moved = lax.all_to_all(part, ('ha', 'wh'), 0, 0, tiled=True)  15.6 us
    ppermute x4, starting transfers between devices, neighbours(): return (lax.ppermute(before, axes, up), lax.ppermute(after, axes, down))  9.08 us
    unnamed x29, local copies, waits for them, and re-layouts  4.05 us
  transfers between devices with their start and end apart: 5, of which 2 were waited for; matrix products, arithmetic and copies ran while one was open for 5% of the time, Pallas kernels for 0%

profile of v1, /device:TPU:0, one launch (start us, length us, event | category | flops | bytes accessed | tf_op | source)
XLA Modules:
  0.0 133.7 jit_solution(7216529896667378381)
XLA Ops:
  0.0 0.8 fusion.1
  0.8 3.5 %collective-permute-start = (bf16[1,64,256]{2,1,0:T(8,128)(2,1)S(1)}, bf16[1,64,256]{2,1,0:T(8,128)(2,1)S(1)}, u32[]{:S(2)}, u32[]{:S(2)}) collective-permute-start(bf16[1,64,256]{2,1,0:T(8,128)(2,1)S(1)} %get-tuple-element.8), channel_id=1, source_target_pairs={{0,16},{16,32},{32,48},{48,64},{64,80},{80,96},{96,112},{1,17},{17... | collective-permute-start | bytes 98312 | tf_op jit(solution)/shard_map/ppermute | solution.py:409
  4.3 1.3 collective-permute-start.1
  5.6 1.1 fusion
  6.7 1.0 fusion.3
  7.7 0.1 copy.27
  7.9 0.7 maximum_bitcast_fusion.rest_2_
  8.7 1.3 %collective-permute-done.1.below_ref = bf16[1,64,256]{2,1,0:T(8,128)(2,1)S(1)} collective-permute-done((bf16[1,64,256]{2,1,0:T(8,128)(2,1)S(1)}, bf16[1,64,256]{2,1,0:T(8,128)(2,1)S(1)}, u32[]{:S(2)}, u32[]{:S(2)}) %collective-permute-start.1) | collective-permute-done | bytes 32800 | tf_op jit(solution)/shard_map/ppermute | solution.py:409
  10.1 1.3 collective-permute-start.3
  11.4 3.0 %collective-permute-start.2 = (bf16[50,256]{1,0:T(8,128)(2,1)S(1)}, bf16[50,256]{1,0:T(8,128)(2,1)S(1)}, u32[]{:S(2)}, u32[]{:S(2)}) collective-permute-start(bf16[50,256]{1,0:T(8,128)(2,1)S(1)} %pad_maximum_fusion), channel_id=1, source_target_pairs={{0,1},{1,2},{2,3},{3,4},{4,5},{5,6},{6,7},{7,8},{8,9},{9,10},{10,1... | collective-permute-start | bytes 76808 | tf_op jit(solution)/shard_map/ppermute | solution.py:409
  14.5 0.7 pad_add_fusion.index_ref
  15.2 0.6 pad.7.table_ref
  15.8 0.6 copy-done.6
  16.4 0.6 copy-done.7
  17.0 30.9 %local_stage.1 = bf16[48,64,256]{2,1,0:T(8,128)(2,1)} custom-call(bf16[48,64,256]{2,1,0:T(8,128)(2,1)} %x_ref.1, bf16[1,64,256]{2,1,0:T(8,128)(2,1)} %copy-done.2, bf16[1,64,256]{2,1,0:T(8,128)(2,1)} %copy-done.3, bf16[50,256]{1,0:T(8,128)(2,1)} %copy-done.7, bf16[50,256]{1,0:T(8,128)(2,1)} %copy-done.6, bf16[256,1024]{1,0:T(8,128)(2,1)} %ew_ref.1, ...), custom_call_target="tpu_custom_call" | custom-call | tf_op jit(solution)/shard_map/local_stage/pallas_call | solution.py:362
  47.9 15.6 %all-to-all-start = ((bf16[64,48,256]{2,1,0:T(8,128)(2,1)}), bf16[64,48,256]{2,1,0:T(8,128)(2,1)S(1)}, u32[]{:S(2)}, u32[]{:S(2)}) async-start(bf16[64,48,256]{2,1,0:T(8,128)(2,1)} %bitcast.25), calls=%async_computation | async-start | bytes 3145728 | tf_op jit(solution)/shard_map/all_to_all | solution.py:433
  63.8 0.6 pad.8.table_ref
  64.4 0.7 pad_add_fusion.1.index_ref
  65.1 0.7 maximum_bitcast_fusion.1.wt_ref
  65.8 20.1 %all-to-all-done.x_ref = bf16[64,48,256]{2,1,0:T(8,128)(2,1)S(1)} async-done(((bf16[64,48,256]{2,1,0:T(8,128)(2,1)}), bf16[64,48,256]{2,1,0:T(8,128)(2,1)S(1)}, u32[]{:S(2)}, u32[]{:S(2)}) %all-to-all-start) | async-done | bytes 1572896 | tf_op jit(solution)/shard_map/all_to_all | solution.py:433
  86.0 1.1 copy-done
  87.1 18.0 %grid_stage.1 = bf16[64,48,256]{2,1,0:T(8,128)(2,1)} custom-call(bf16[64,48,256]{2,1,0:T(8,128)(2,1)} %copy-done, bf16[256,768]{1,0:T(8,128)(2,1)} %qkv_ref.1, bf16[512,256]{1,0:T(8,128)(2,1)} %maximum_bitcast_fusion.1.wt_ref, f32[8,256]{1,0:T(8,128)} %pad.8.table_ref, s32[64,128]{1,0:T(8,128)} %pad_add_fusion.1.index_ref, bf16[256,256]{1,0:T(8,128)(2,1)} %late0_ref.1, ...), custom_call_target="tpu_custom_call" | custom-call | tf_op jit(solution)/shard_map/grid_stage/pallas_call | solution.py:382
  105.1 27.5 %all_to_all.10 = bf16[64,48,256]{2,1,0:T(8,128)(2,1)S(1)} all-to-all(bf16[64,48,256]{2,1,0:T(8,128)(2,1)} %grid_stage.1), channel_id=1, replica_groups=mesh['ha'=8,'wh'=8,'core'=2] {'ha','wh'}, dimensions={0} | all-to-all | bytes 3145728 | tf_op jit(solution)/shard_map/all_to_all | solution.py:435
  132.6 1.1 copy.36
  (32 shorter events, 0.6 us)
Async XLA Ops:
  0.0 8.6 %copy-start.4 = (s32[64,64]{1,0:T(8,128)S(1)}, s32[64,64]{1,0:T(8,128)}, u32[]{:S(2)}) copy-start(s32[64,64]{1,0:T(8,128)} %param.23) | copy-start | bytes 49156
  0.0 15.2 %copy-start.8 = (f32[225,8]{0,1:T(8,128)S(1)}, f32[225,8]{0,1:T(8,128)}, u32[]{:S(2)}) copy-start(f32[225,8]{0,1:T(8,128)} %param.22) | copy-start | bytes 21604
  0.8 7.9 %collective-permute-start = (bf16[1,64,256]{2,1,0:T(8,128)(2,1)S(1)}, bf16[1,64,256]{2,1,0:T(8,128)(2,1)S(1)}, u32[]{:S(2)}, u32[]{:S(2)}) collective-permute-start(bf16[1,64,256]{2,1,0:T(8,128)(2,1)S(1)} %get-tuple-element.8), channel_id=1, source_target_pairs={{0,16},{16,32},{32,48},{48,64},{64,80},{80,96},{96,112},{1,17},{17... | collective-permute-start | bytes 98312 | tf_op jit(solution)/shard_map/ppermute | solution.py:409
  4.3 5.8 %collective-permute-start.1 = (bf16[1,64,256]{2,1,0:T(8,128)(2,1)S(1)}, bf16[1,64,256]{2,1,0:T(8,128)(2,1)S(1)}, u32[]{:S(2)}, u32[]{:S(2)}) collective-permute-start(bf16[1,64,256]{2,1,0:T(8,128)(2,1)S(1)} %get-tuple-element.7), channel_id=1, source_target_pairs={{16,0},{32,16},{48,32},{64,48},{80,64},{96,80},{112,96},{17,1},{33... | collective-permute-start | bytes 98312 | tf_op jit(solution)/shard_map/ppermute | solution.py:409
  8.7 7.1 %copy-start.2 = (bf16[1,64,256]{2,1,0:T(8,128)(2,1)}, bf16[1,64,256]{2,1,0:T(8,128)(2,1)S(1)}, u32[]{:S(2)}) copy-start(bf16[1,64,256]{2,1,0:T(8,128)(2,1)S(1)} %collective-permute-done.above_ref) | copy-start | bytes 98308
  10.1 5.7 %copy-start.3 = (bf16[1,64,256]{2,1,0:T(8,128)(2,1)}, bf16[1,64,256]{2,1,0:T(8,128)(2,1)S(1)}, u32[]{:S(2)}) copy-start(bf16[1,64,256]{2,1,0:T(8,128)(2,1)S(1)} %collective-permute-done.1.below_ref) | copy-start | bytes 98308
  10.1 5.6 %collective-permute-start.3 = (bf16[50,256]{1,0:T(8,128)(2,1)S(1)}, bf16[50,256]{1,0:T(8,128)(2,1)S(1)}, u32[]{:S(2)}, u32[]{:S(2)}) collective-permute-start(bf16[50,256]{1,0:T(8,128)(2,1)S(1)} %pad_maximum_fusion.1), channel_id=1, source_target_pairs={{1,0},{2,1},{3,2},{4,3},{5,4},{6,5},{7,6},{8,7},{9,8},{10,9},{11,1... | collective-permute-start | bytes 76808 | tf_op jit(solution)/shard_map/ppermute | solution.py:409
  11.4 4.3 %collective-permute-start.2 = (bf16[50,256]{1,0:T(8,128)(2,1)S(1)}, bf16[50,256]{1,0:T(8,128)(2,1)S(1)}, u32[]{:S(2)}, u32[]{:S(2)}) collective-permute-start(bf16[50,256]{1,0:T(8,128)(2,1)S(1)} %pad_maximum_fusion), channel_id=1, source_target_pairs={{0,1},{1,2},{2,3},{3,4},{4,5},{5,6},{6,7},{7,8},{8,9},{9,10},{10,1... | collective-permute-start | bytes 76808 | tf_op jit(solution)/shard_map/ppermute | solution.py:409
  15.8 0.6 copy-start.6
  16.4 0.6 copy-start.7
  47.9 15.6 %copy-start.1 = (bf16[256,768]{1,0:T(8,128)(2,1)S(1)}, bf16[256,768]{1,0:T(8,128)(2,1)}, u32[]{:S(2)}) copy-start(bf16[256,768]{1,0:T(8,128)(2,1)} %qkv_ref.1) | copy-start | bytes 1179652
  47.9 15.9 %copy-start.5 = (s32[64,64]{1,0:T(8,128)S(1)}, s32[64,64]{1,0:T(8,128)}, u32[]{:S(2)}) copy-start(s32[64,64]{1,0:T(8,128)} %param.29) | copy-start | bytes 49156
  47.9 15.9 %copy-start.9 = (f32[225,8]{0,1:T(8,128)S(1)}, f32[225,8]{0,1:T(8,128)}, u32[]{:S(2)}) copy-start(f32[225,8]{0,1:T(8,128)} %param.28) | copy-start | bytes 21604
  47.9 38.0 %all-to-all-start = ((bf16[64,48,256]{2,1,0:T(8,128)(2,1)}), bf16[64,48,256]{2,1,0:T(8,128)(2,1)S(1)}, u32[]{:S(2)}, u32[]{:S(2)}) async-start(bf16[64,48,256]{2,1,0:T(8,128)(2,1)} %bitcast.25), calls=%async_computation | async-start | bytes 3145728 | tf_op jit(solution)/shard_map/all_to_all | solution.py:433
  86.0 1.1 copy-start

commit v2 on v1

--- a/solution.py
+++ b/solution.py
@@ -173,20 +173,21 @@
         y_ref[rows] = x_ref[rows] + 0.5 * mm(g_ref[...], down_ref[...])
         return carry
 
-    lax.fori_loop(0, 2, half, 0)
+    half(0, 0)
+    half(1, 0)
 
 
 def local_kernel(
     first, strips,
     x_ref, above_ref, below_ref, left_ref, right_ref,
-    ew_ref, dw_ref, table_ref, index_ref, *rest
+    table_ref, index_ref, *rest
 ):
-    late, rest = rest[:6], rest[6:]
+    late, rest = rest[:7], rest[7:]
     res_ref, hid_ref, act_ref, xn_ref, sems = rest[:5]
-    pw_ref, qkv_ref, wt_ref, out_w_ref, up_ref, down_ref = rest[5:11]
-    bias_ref, xw_ref, n_ref, k_ref, qvt_ref, o_ref, g_ref, y_ref = rest[11:19]
-    units = rest[19:]
-    copies = fetch(late, rest[5:11], sems)
+    ew_ref, dw_ref, pw_ref, qkv_ref, out_w_ref, up_ref, down_ref, wt_ref = rest[5:13]
+    bias_ref, xw_ref, n_ref, k_ref, qvt_ref, o_ref, g_ref, y_ref = rest[13:21]
+    units = rest[21:]
+    copies = fetch(late, rest[5:12], sems)
     rows = 8 * strips
     last = x_ref.shape[0]
     make_bias(table_ref, index_ref, bias_ref)
@@ -248,6 +249,8 @@
                 lanes = slice(256 * p + 128 * c, 256 * p + 128 * c + 128)
                 act_ref[pl.ds(to, 32), lanes] = gelu2(acc[ir - 2])
 
+    for copy in copies[:2]:
+        copy.wait()
     for p in range(4):
         hidden_border(p)
 
@@ -280,13 +283,15 @@
             n_ref[to] = norm(x)
         return carry
 
-    copies[0].wait()
+    copies[2].wait()
     lax.fori_loop(0, 2, project, 0)
     lax.fori_loop(0, strips, gather, 0)
-    for copy in copies[1:3]:
-        copy.wait()
+    copies[3].wait()
+    for i in range(2):
+        turned_map = qkv_ref[:, 512 * i : 512 * i + 256].astype(F32).T
+        wt_ref[256 * i : 256 * i + 256] = turned_map.astype(BF16)
     attend(8 * strips, n_ref, qkv_ref, wt_ref, bias_ref, k_ref, qvt_ref, o_ref, units[:UNITS], units[UNITS : 2 * UNITS], units[2 * UNITS :])
-    for copy in copies[3:]:
+    for copy in copies[4:]:
         copy.wait()
     project_and_feed(xw_ref, o_ref, g_ref, n_ref, out_w_ref, up_ref, down_ref, y_ref)
 
@@ -344,6 +349,10 @@
     ] + [pltpu.VMEM(shape, kind) for shape, kind in UNIT_SCRATCH for _ in range(UNITS)]
 
 
+def on_chip(arrays):
+    return tuple(pltpu.with_memory_space_constraint(a, pltpu.VMEM) for a in arrays)
+
+
 def landing(arrays):
     return [pltpu.SemaphoreType.DMA((len(arrays),))] + [pltpu.VMEM(a.shape, a.dtype) for a in arrays]
 
@@ -370,6 +379,7 @@
             pltpu.VMEM((64 * rows + 256, 256), BF16),
         ]
         + landing(late)
+        + [pltpu.VMEM((512, 256), BF16)]
         + attend_scratch(8 * strips),
         compiler_params=PARAMS,
         name="local_stage",
@@ -419,19 +429,20 @@
     first = jnp.concatenate([above[:, 0], field[:, 0], below[:, 0]], axis=0)
     final = jnp.concatenate([above[:, -1], field[:, -1], below[:, -1]], axis=0)
     left, right = neighbours(final, first, ("wh", "core"))
-    cells = (field, above, below, left, right)
-    local_w = (expand_w, dw_kernel) + bias_operands(blk_table, blk_index)
-    local_late = (project_w, blk_qkv, turned(blk_qkv), blk_out, blk_up, blk_down)
+    cells = (field,) + on_chip((above, below, left, right))
+    local_w = bias_operands(blk_table, blk_index)
+    local_late = (expand_w, dw_kernel, project_w, blk_qkv, blk_out, blk_up, blk_down)
     grid_w = (grid_qkv, turned(grid_qkv)) + bias_operands(grid_table, grid_index)
     grid_late = (grid_out, grid_up, grid_down)
     outs = []
     start = 0
     for strips in CHUNKS:
-        part = local_stage(start, strips, cells, local_w, local_late)
+        part = local_stage(start, strips, cells, on_chip(local_w), local_late)
         start += strips
         part = part.reshape(64, strips * 8, width)
         moved = lax.all_to_all(part, ("ha", "wh"), 0, 0, tiled=True)
-        done = grid_stage(moved, grid_w, grid_late)
+        (moved,) = on_chip((moved,))
+        done = grid_stage(moved, on_chip(grid_w), grid_late)
         back = lax.all_to_all(done, ("ha", "wh"), 0, 0, tiled=True)
         outs.append(back.reshape(strips * 8, cols, width))
     return outs[0] if len(outs) == 1 else jnp.concatenate(outs, axis=0)

time: 134 us -> 129 us (0.963)
  local copies, waits for them, and re-layouts: 8.15 us -> 4.91 us
  other arithmetic: 2.82 us -> 0.2 us
  Pallas kernels: 48.9 us -> 46.6 us
  waiting for transfers between devices: 21.5 us -> 23.4 us
    pallas_call x1, Pallas kernels: 18 us -> 15.6 us  [grid_stage(): pl.pallas_call(functools.partial(grid_kernel, windows), in_specs=in_vmem(...]
    unnamed x29 -> x13, local copies, waits for them, and re-layouts: 4.05 us -> 2.28 us
    transpose x2 -> x1, other arithmetic: 1.42 us -> 0.02 us  [turned(): return jnp.concatenate([qkv[:, :256], qkv[:, 512:]], axis=1).T]
  transfers between devices with their start and end apart: 5 -> 5, of which waited for: 2 -> 2; matrix products, arithmetic and copies ran while one was open for 5% -> 2% of each run, Pallas kernels for 0% -> 0%
where the time goes in v2:
time: 129 us
  Pallas kernels  46.6 us (36%)
  blocking collectives  27.6 us (21%)
  starting transfers between devices  25.9 us (20%)
  waiting for transfers between devices  23.4 us (18%)
  local copies, waits for them, and re-layouts  4.91 us (4%)
    pallas_call x1, Pallas kernels, local_stage(): pl.pallas_call(functools.partial(local_kernel, first, strips), in_specs=i...  30.9 us
    all_to_all x1, blocking collectives, on_device(): back = lax.all_to_all(done, ('ha', 'wh'), 0, 0, tiled=True)  27.6 us
    all_to_all x1, waiting for transfers between devices, on_device(): moved = lax.all_to_all(part, ('ha', 'wh'), 0, 0, tiled=True)  20.9 us
    all_to_all x1, starting transfers between devices, on_device(): moved = lax.all_to_all(part, ('ha', 'wh'), 0, 0, tiled=True)  16.8 us
    pallas_call x1, Pallas kernels, grid_stage(): pl.pallas_call(functools.partial(grid_kernel, windows), in_specs=in_vmem(...  15.6 us
    ppermute x4, starting transfers between devices, neighbours(): return (lax.ppermute(before, axes, up), lax.ppermute(after, axes, down))  9.08 us
  transfers between devices with their start and end apart: 5, of which 2 were waited for; matrix products, arithmetic and copies ran while one was open for 2% of the time, Pallas kernels for 0%

profile of v2, /device:TPU:0, one launch (start us, length us, event | category | flops | bytes accessed | tf_op | source)
XLA Modules:
  0.0 128.8 jit_solution(3509213249624352174)
XLA Ops:
  0.0 0.8 fusion.1
  0.8 3.5 %collective-permute-start = (bf16[1,64,256]{2,1,0:T(8,128)(2,1)S(1)}, bf16[1,64,256]{2,1,0:T(8,128)(2,1)S(1)}, u32[]{:S(2)}, u32[]{:S(2)}) collective-permute-start(bf16[1,64,256]{2,1,0:T(8,128)(2,1)S(1)} %get-tuple-element.8), channel_id=1, source_target_pairs={{0,16},{16,32},{32,48},{48,64},{64,80},{80,96},{96,112},{1,17},{17... | collective-permute-start | bytes 98312 | tf_op jit(solution)/shard_map/ppermute | solution.py:419
  4.3 1.3 %collective-permute-start.1 = (bf16[1,64,256]{2,1,0:T(8,128)(2,1)S(1)}, bf16[1,64,256]{2,1,0:T(8,128)(2,1)S(1)}, u32[]{:S(2)}, u32[]{:S(2)}) collective-permute-start(bf16[1,64,256]{2,1,0:T(8,128)(2,1)S(1)} %get-tuple-element.7), channel_id=1, source_target_pairs={{16,0},{32,16},{48,32},{64,48},{80,64},{96,80},{112,96},{17,1},{33... | collective-permute-start | bytes 98312 | tf_op jit(solution)/shard_map/ppermute | solution.py:419
  5.6 1.1 fusion
  6.7 0.8 copy.19
  7.6 2.5 %collective-permute-done.1.below_ref = bf16[1,64,256]{2,1,0:T(8,128)(2,1)S(1)} collective-permute-done((bf16[1,64,256]{2,1,0:T(8,128)(2,1)S(1)}, bf16[1,64,256]{2,1,0:T(8,128)(2,1)S(1)}, u32[]{:S(2)}, u32[]{:S(2)}) %collective-permute-start.1) | collective-permute-done | bytes 32800 | tf_op jit(solution)/shard_map/ppermute | solution.py:419
  10.1 1.3 %collective-permute-start.3 = (bf16[50,256]{1,0:T(8,128)(2,1)S(1)}, bf16[50,256]{1,0:T(8,128)(2,1)S(1)}, u32[]{:S(2)}, u32[]{:S(2)}) collective-permute-start(bf16[50,256]{1,0:T(8,128)(2,1)S(1)} %pad_maximum_fusion.1), channel_id=1, source_target_pairs={{1,0},{2,1},{3,2},{4,3},{5,4},{6,5},{7,6},{8,7},{9,8},{10,9},{11,1... | collective-permute-start | bytes 76808 | tf_op jit(solution)/shard_map/ppermute | solution.py:419
  11.4 3.0 %collective-permute-start.2 = (bf16[50,256]{1,0:T(8,128)(2,1)S(1)}, bf16[50,256]{1,0:T(8,128)(2,1)S(1)}, u32[]{:S(2)}, u32[]{:S(2)}) collective-permute-start(bf16[50,256]{1,0:T(8,128)(2,1)S(1)} %pad_maximum_fusion), channel_id=1, source_target_pairs={{0,1},{1,2},{2,3},{3,4},{4,5},{5,6},{6,7},{7,8},{8,9},{9,10},{10,1... | collective-permute-start | bytes 76808 | tf_op jit(solution)/shard_map/ppermute | solution.py:419
  14.5 0.1 pad_add_fusion.index_ref
  14.5 0.7 pad.7.table_ref
  15.2 0.0 collective-permute-done.2.left_ref
  15.3 30.9 %local_stage.1 = bf16[48,64,256]{2,1,0:T(8,128)(2,1)} custom-call(bf16[48,64,256]{2,1,0:T(8,128)(2,1)} %x_ref.1, bf16[1,64,256]{2,1,0:T(8,128)(2,1)S(1)} %collective-permute-done.above_ref, bf16[1,64,256]{2,1,0:T(8,128)(2,1)S(1)} %collective-permute-done.1.below_ref, bf16[50,256]{1,0:T(8,128)(2,1)S(1)} %collective-permute-done.2.left_ref, ...), custom_call_target="tpu_custom_call" | custom-call | tf_op jit(solution)/shard_map/local_stage/pallas_call | solution.py:371
  46.2 0.0 copy-start
  46.2 0.0 copy-start.1
  46.3 0.0 copy-start.2
  46.3 16.8 %all-to-all-start = ((bf16[64,48,256]{2,1,0:T(8,128)(2,1)}), bf16[64,48,256]{2,1,0:T(8,128)(2,1)S(1)}, u32[]{:S(2)}, u32[]{:S(2)}) async-start(bf16[64,48,256]{2,1,0:T(8,128)(2,1)} %bitcast.23), calls=%async_computation | async-start | bytes 3145728 | tf_op jit(solution)/shard_map/all_to_all | solution.py:443
  63.1 0.1 copy.25
  63.3 0.1 copy.26
  63.4 0.1 copy.22
  63.5 0.1 pad_add_fusion.1.index_ref
  63.6 20.9 %all-to-all-done.x_ref = bf16[64,48,256]{2,1,0:T(8,128)(2,1)S(1)} async-done(((bf16[64,48,256]{2,1,0:T(8,128)(2,1)}), bf16[64,48,256]{2,1,0:T(8,128)(2,1)S(1)}, u32[]{:S(2)}, u32[]{:S(2)}) %all-to-all-start) | async-done | bytes 1572896 | tf_op jit(solution)/shard_map/all_to_all | solution.py:443
  84.4 15.6 %grid_stage.1 = bf16[64,48,256]{2,1,0:T(8,128)(2,1)} custom-call(bf16[64,48,256]{2,1,0:T(8,128)(2,1)S(1)} %all-to-all-done.x_ref, bf16[256,768]{1,0:T(8,128)(2,1)S(1)} %copy-done, bf16[512,256]{1,0:T(8,128)(2,1)S(1)} %maximum_bitcast_fusion.wt_ref, f32[8,256]{1,0:T(8,128)S(1)} %pad.8.table_ref, s32[64,128]{1,0:T(8,128)S(1)} %pad_add_fusion.1.index_ref, ...), custom_call_target="tpu_custom_call" | custom-call | tf_op jit(solution)/shard_map/grid_stage/pallas_call | solution.py:392
  100.1 27.6 %all_to_all.10 = bf16[64,48,256]{2,1,0:T(8,128)(2,1)S(1)} all-to-all(bf16[64,48,256]{2,1,0:T(8,128)(2,1)} %grid_stage.1), channel_id=1, replica_groups=mesh['ha'=8,'wh'=8,'core'=2] {'ha','wh'}, dimensions={0} | all-to-all | bytes 3145728 | tf_op jit(solution)/shard_map/all_to_all | solution.py:446
  127.7 1.1 copy.32
  (14 shorter events, 0.1 us)
Async XLA Ops:
  0.8 6.8 %collective-permute-start = (bf16[1,64,256]{2,1,0:T(8,128)(2,1)S(1)}, bf16[1,64,256]{2,1,0:T(8,128)(2,1)S(1)}, u32[]{:S(2)}, u32[]{:S(2)}) collective-permute-start(bf16[1,64,256]{2,1,0:T(8,128)(2,1)S(1)} %get-tuple-element.8), channel_id=1, source_target_pairs={{0,16},{16,32},{32,48},{48,64},{64,80},{80,96},{96,112},{1,17},{17... | collective-permute-start | bytes 98312 | tf_op jit(solution)/shard_map/ppermute | solution.py:419
  4.3 5.8 %collective-permute-start.1 = (bf16[1,64,256]{2,1,0:T(8,128)(2,1)S(1)}, bf16[1,64,256]{2,1,0:T(8,128)(2,1)S(1)}, u32[]{:S(2)}, u32[]{:S(2)}) collective-permute-start(bf16[1,64,256]{2,1,0:T(8,128)(2,1)S(1)} %get-tuple-element.7), channel_id=1, source_target_pairs={{16,0},{32,16},{48,32},{64,48},{80,64},{96,80},{112,96},{17,1},{33... | collective-permute-start | bytes 98312 | tf_op jit(solution)/shard_map/ppermute | solution.py:419
  10.1 5.1 %collective-permute-start.3 = (bf16[50,256]{1,0:T(8,128)(2,1)S(1)}, bf16[50,256]{1,0:T(8,128)(2,1)S(1)}, u32[]{:S(2)}, u32[]{:S(2)}) collective-permute-start(bf16[50,256]{1,0:T(8,128)(2,1)S(1)} %pad_maximum_fusion.1), channel_id=1, source_target_pairs={{1,0},{2,1},{3,2},{4,3},{5,4},{6,5},{7,6},{8,7},{9,8},{10,9},{11,1... | collective-permute-start | bytes 76808 | tf_op jit(solution)/shard_map/ppermute | solution.py:419
  11.4 3.9 %collective-permute-start.2 = (bf16[50,256]{1,0:T(8,128)(2,1)S(1)}, bf16[50,256]{1,0:T(8,128)(2,1)S(1)}, u32[]{:S(2)}, u32[]{:S(2)}) collective-permute-start(bf16[50,256]{1,0:T(8,128)(2,1)S(1)} %pad_maximum_fusion), channel_id=1, source_target_pairs={{0,1},{1,2},{2,3},{3,4},{4,5},{5,6},{6,7},{7,8},{8,9},{9,10},{10,1... | collective-permute-start | bytes 76808 | tf_op jit(solution)/shard_map/ppermute | solution.py:419
  46.2 16.9 %copy-start = (bf16[256,768]{1,0:T(8,128)(2,1)S(1)}, bf16[256,768]{1,0:T(8,128)(2,1)}, u32[]{:S(2)}) copy-start(bf16[256,768]{1,0:T(8,128)(2,1)} %qkv_ref.1) | copy-start | bytes 1179652
  46.2 17.1 %copy-start.1 = (s32[64,64]{1,0:T(8,128)S(1)}, s32[64,64]{1,0:T(8,128)}, u32[]{:S(2)}) copy-start(s32[64,64]{1,0:T(8,128)} %param.29) | copy-start | bytes 49156
  46.3 17.2 %copy-start.2 = (f32[225,8]{0,1:T(8,128)S(1)}, f32[225,8]{0,1:T(8,128)}, u32[]{:S(2)}) copy-start(f32[225,8]{0,1:T(8,128)} %param.28) | copy-start | bytes 21604
  46.3 38.2 %all-to-all-start = ((bf16[64,48,256]{2,1,0:T(8,128)(2,1)}), bf16[64,48,256]{2,1,0:T(8,128)(2,1)S(1)}, u32[]{:S(2)}, u32[]{:S(2)}) async-start(bf16[64,48,256]{2,1,0:T(8,128)(2,1)} %bitcast.23), calls=%async_computation | async-start | bytes 3145728 | tf_op jit(solution)/shard_map/all_to_all | solution.py:443
